TPU v7x, 32 devices: a whole 2x2x4 slice. The times are simulated.
32 devices in a mesh: dp: 4 (over z), mp: 8 (over y, x, core).
Axes of the slice: x: 2, y: 2, z: 4, core: 2. Of those that a mesh axis runs over, the one named last changes fastest.
Arguments:
- hidden_in: bfloat16 [64, 8192], P(None, 'dp'), may hold values from -25 to 25
- norm_gain: bfloat16 [8192], P('dp'), may hold values from 0.099609375 to 1.8984375
- w_query: bfloat16 [8192, 8192], P('dp', 'mp'), may hold values from -0.0625 to 0.0625
- w_keyval: bfloat16 [8192, 2048], P('dp', 'mp'), may hold values from -0.25 to 0.25
- w_out: bfloat16 [8192, 8192], P('mp', 'dp'), may hold values from -0.5 to 0.5
- cache_slots: bfloat16 [2, 64, 2, 8, 512, 128], P(None, ('dp', 'mp')), may hold values from -140 to 140
- lengths: int32 [64], replicated, may hold values from 1 to 512, 16384 in all
- positions: int32 [64], replicated, may hold values from 0 to 8191
- slot_order: int32 [64], replicated, may hold values from 0 to 63, each once
Outputs:
- result: bfloat16 [64, 8192], P(None, 'dp')
Inputs may be any that keep to these rules, and one draw needn't show every extreme that they name: `lengths`: every request has at least one valid cache position; the longest has 512. `slot_order`: each request's cache sits in exactly one slot.
All inputs are finite; a program needn't handle non-finite values.
Results may differ from a plain program's by a relative error of at most 0.035.
Values may be sent and summed in bfloat16 or wider, within the bound.
A program may use at most 128 MiB of HBM per device.

v0:
```python
import math

import jax
import jax.numpy as jnp
from jax import lax
from jax.sharding import PartitionSpec as P

LAYERS = 2


norm_eps = 1e-05
rope_base = 500000.0


def rotate(values, at_positions):
    half_dim = values.shape[-1] // 2
    index_row = jnp.arange(half_dim, dtype=jnp.float32)
    frequency = jnp.exp(index_row * (-2.0 * math.log(rope_base) / values.shape[-1]))
    angles = at_positions.astype(jnp.float32)[:, None, None] * frequency
    cosines = jnp.cos(angles)
    sine_rows = jnp.sin(angles)
    first_half = values[..., :half_dim]
    second_half = values[..., half_dim:]
    return jnp.concatenate(
        [
            first_half * cosines - second_half * sine_rows,
            second_half * cosines + first_half * sine_rows,
        ],
        axis=-1,
    )


def attend(queries, fresh_keys, fresh_values, key_rows, values, slot_lengths):
    score_scale = 1.0 / math.sqrt(queries.shape[-1])
    scores = (
        jnp.einsum("rkgd,rktd->rkgt", queries, key_rows, preferred_element_type=jnp.float32)
        * score_scale
    )
    own_score = (
        jnp.einsum("rkgd,rkd->rkg", queries, fresh_keys, preferred_element_type=jnp.float32)
        * score_scale
    )
    positions_row = lax.broadcasted_iota(jnp.int32, (1, 1, 1, key_rows.shape[2]), 3)
    valid_keys = positions_row < slot_lengths[:, None, None, None]
    scores = jnp.where(valid_keys, scores, -jnp.inf)
    highest = jnp.maximum(jnp.max(scores, axis=-1), own_score)
    weights = jnp.exp(scores - highest[..., None])
    own_weight = jnp.exp(own_score - highest)
    denominator = jnp.sum(weights, axis=-1) + own_weight
    rounded = weights.astype(jnp.bfloat16)
    own_rounded = lax.optimization_barrier(own_weight.astype(jnp.bfloat16)).astype(jnp.float32)
    summed = jnp.einsum("rkgt,rktd->rkgd", rounded, values, preferred_element_type=jnp.float32)
    summed = summed + own_rounded[..., None] * fresh_values.astype(jnp.float32)[:, :, None, :]
    return (summed / denominator[..., None]).astype(jnp.bfloat16)


def shards(
    hidden_in, norm_gain, w_query, w_keyval, w_out, cache_slots, lengths, positions, slot_order
):
    total_rows = hidden_in.shape[0]
    data_count = lax.axis_size("dp")
    model_count = lax.axis_size("mp")
    owned_rows = cache_slots.shape[1]
    key_heads = cache_slots.shape[3]
    head_dim = cache_slots.shape[5]
    query_cols = w_query.shape[1]
    head_count = query_cols * model_count // head_dim
    group_size = head_count // key_heads
    model_width = hidden_in.shape[1] * data_count
    half_width = key_heads * head_dim
    inverse = (
        jnp.zeros((total_rows,), jnp.int32)
        .at[slot_order]
        .set(jnp.arange(total_rows, dtype=jnp.int32))
    )
    device_index = lax.axis_index("dp") * model_count + lax.axis_index("mp")
    slot_lengths = lax.dynamic_slice_in_dim(
        jnp.take(lengths, slot_order), device_index * owned_rows, owned_rows
    )
    slot_positions = lax.dynamic_slice_in_dim(
        jnp.take(positions, slot_order), device_index * owned_rows, owned_rows
    )
    gain_float = norm_gain.astype(jnp.float32)
    current = jnp.take(hidden_in, slot_order, axis=0)
    for layer_index in range(LAYERS):
        floats = current.astype(jnp.float32)
        squares = jnp.sum(floats * floats, axis=1)
        scaled = (floats * gain_float).astype(jnp.bfloat16)
        partial_value = jnp.concatenate(
            [
                jnp.dot(scaled, w_query, preferred_element_type=jnp.float32),
                jnp.dot(scaled, w_keyval, preferred_element_type=jnp.float32),
            ],
            axis=1,
        )
        summed = lax.psum_scatter(partial_value, "dp", scatter_dimension=0, tiled=True)
        square_sum = lax.psum_scatter(squares, "dp", scatter_dimension=0, tiled=True)
        inverse_rms = lax.rsqrt(square_sum / model_width + norm_eps)
        projected = summed * inverse_rms[:, None]
        arrived = lax.all_to_all(projected, "mp", split_axis=0, concat_axis=1, tiled=True)
        arrived = arrived.reshape(owned_rows, model_count, projected.shape[1])
        query_part = arrived[:, :, :query_cols].reshape(owned_rows, head_count, head_dim)
        keyval_part = arrived[:, :, query_cols:].reshape(owned_rows, 2 * half_width)
        queries = (
            rotate(query_part, slot_positions)
            .astype(jnp.bfloat16)
            .reshape(owned_rows, key_heads, group_size, head_dim)
        )
        fresh_keys = rotate(
            keyval_part[:, :half_width].reshape(owned_rows, key_heads, head_dim), slot_positions
        ).astype(jnp.bfloat16)
        fresh_values = (
            keyval_part[:, half_width:]
            .reshape(owned_rows, key_heads, head_dim)
            .astype(jnp.bfloat16)
        )
        layer_cache = cache_slots[layer_index]
        attended = attend(
            queries, fresh_keys, fresh_values, layer_cache[:, 0], layer_cache[:, 1], slot_lengths
        )
        attended = attended.reshape(owned_rows, head_count * head_dim)
        returned = lax.all_to_all(attended, "mp", split_axis=1, concat_axis=0, tiled=True)
        partial_out = jnp.dot(
            lax.all_gather(returned, "dp", axis=0, tiled=True),
            w_out,
            preferred_element_type=jnp.float32,
        )
        totals = lax.psum(partial_out, "mp")
        current = (floats + totals).astype(jnp.bfloat16)
    return jnp.take(current, inverse, axis=0)


def solution(mesh):
    placed = (
        P(None, "dp"),
        P("dp"),
        P("dp", "mp"),
        P("dp", "mp"),
        P("mp", "dp"),
        P(None, ("dp", "mp"), None, None, None, None),
        P(),
        P(),
        P(),
    )
    return jax.shard_map(
        shards, mesh=mesh, in_specs=placed, out_specs=P(None, "dp"), check_vma=False
    )
```

profile of v0, /device:TPU:0, one launch (start us, length us, event | category | flops | bytes accessed | tf_op | source)
XLA Modules:
  0.0 262.7 jit_solution(91832775183974861)
XLA Ops:
  12.4 3.1 %fusion.30 = f32[64,1024]{1,0:T(8,128)S(1)} fusion(bf16[2048,1024]{1,0:T(8,128)(2,1)} %param.15, f32[2048]{0:T(1024)S(1)} %convert_element_type.90, bf16[64,2048]{1,0:T(8,128)(2,1)S(1)} %gather_fusion, pred[64]{0:T(512)(128)(4,1)S(1)} %get-tuple-element.10), kind=kOutput, calls=%fused_computation.50 | convolution fusion | flops 268959744 | bytes 4726848 | tf_op jit(solution)/shard_map/dot_general | solution.py:91
  16.5 5.9 %fusion.59 = (bf16[1,2,2,8,512,128]{5,4,3,2,1,0:T(8,128)(2,1)}, bf16[1,2,2,8,512,128]{5,4,3,2,1,0:T(8,128)(2,1)}) fusion(bf16[2,2,2,8,512,128]{5,4,3,2,1,0:T(8,128)(2,1)} %param.18), kind=kLoop, calls=%fused_computation.118 | loop fusion | bytes 16777216 | tf_op jit(solution)/shard_map/slice | solution.py:117
  22.4 13.4 %all-reduce = f32[64]{0:T(128)S(1)} all-reduce(f32[64]{0:T(128)S(1)} %fusion.15), channel_id=3, replica_groups=mesh['dp'=4,'mp'=8] {'dp'}, use_global_device_ids=true, to_apply=%region_2.0.clone | all-reduce | flops 64 | bytes 512
  38.2 5.9 %copy_bitcast_fusion = (bf16[2,2,8,512,128]{4,3,2,0,1:T(8,128)(2,1)}, bf16[2,2,8,512,128]{4,3,2,0,1:T(8,128)(2,1)}) fusion(bf16[1,2,2,8,512,128]{5,4,3,2,1,0:T(8,128)(2,1)} %get-tuple-element.12, bf16[1,2,2,8,512,128]{5,4,3,2,1,0:T(8,128)(2,1)} %get-tuple-element.11), kind=kLoop, calls=%fused_computation.5 | loop fusion | bytes 16777216 | tf_op jit(solution)/shard_map/squeeze | solution.py:117
  45.8 3.7 %all-to-all-start = ((f32[8,2,1280]{2,1,0:T(2,128)}), f32[8,2,1280]{2,1,0:T(2,128)S(1)}, u32[]{:S(2)}, u32[]{:S(2)}) async-start(f32[8,2,1280]{2,1,0:T(2,128)} %all_to_all.52), calls=%async_computation.1 | async-start | bytes 163840 | tf_op jit(solution)/shard_map/all_to_all | solution.py:100
  49.6 5.0 %all-to-all-done = f32[8,2,1280]{2,1,0:T(2,128)S(1)} async-done(((f32[8,2,1280]{2,1,0:T(2,128)}), f32[8,2,1280]{2,1,0:T(2,128)S(1)}, u32[]{:S(2)}, u32[]{:S(2)}) %all-to-all-start) | async-done | bytes 81952 | tf_op jit(solution)/shard_map/all_to_all | solution.py:100
  55.2 2.4 fusion.60
  57.8 2.0 fusion.13
  59.9 7.2 %all_to_all.70 = bf16[2,8,1024]{2,0,1:T(2,128)(2,1)S(1)} all-to-all(bf16[2,8,1024]{2,0,1:T(2,128)(2,1)S(1)} %copy.21), channel_id=1, replica_groups=mesh['dp'=4,'mp'=8] {'mp'}, dimensions={1} | all-to-all | bytes 65536 | tf_op jit(solution)/shard_map/all_to_all | solution.py:122
  67.2 13.5 %all_gather.6 = bf16[64,1024]{1,0:T(8,128)(2,1)S(1)} all-gather(bf16[16,1024]{1,0:T(8,128)(2,1)S(1)} %all_to_all.58), channel_id=1, replica_groups=mesh['dp'=4,'mp'=8] {'dp'}, dimensions={0}, use_global_device_ids=true | all-gather | bytes 163840 | tf_op jit(solution)/shard_map/all_gather | solution.py:124
  80.7 3.9 %fusion.62 = f32[64,2048]{1,0:T(8,128)} fusion(bf16[64,1024]{1,0:T(8,128)(2,1)S(1)} %all_gather.6, bf16[1024,2048]{1,0:T(8,128)(2,1)} %param.17), kind=kOutput, calls=%fused_computation.121 | convolution fusion | flops 268435456 | bytes 4849664 | tf_op jit(solution)/shard_map/dot_general | solution.py:123
  84.6 51.1 %all-reduce.5.cloned.1.call-done = f32[64,2048]{1,0:T(8,128)} async-done(((f32[64,2048]{1,0:T(8,128)}), f32[64,2048]{1,0:T(8,128)}) %all-reduce.5.cloned.1.call-update) | async-done | bytes 524304 | tf_op jit(solution)/shard_map/psum | solution.py:128
  137.3 3.0 %fusion.26 = f32[64,1024]{1,0:T(8,128)S(1)} fusion(bf16[2048,1024]{1,0:T(8,128)(2,1)} %param.15, bf16[64,2048]{1,0:T(8,128)(2,1)S(1)} %get-tuple-element.8, f32[2048]{0:T(1024)S(1)} %convert_element_type.90), kind=kOutput, calls=%fused_computation.48 | convolution fusion | flops 268828672 | bytes 4726784 | tf_op jit(solution)/shard_map/dot_general | solution.py:91
  141.1 11.7 %all-reduce.1 = f32[64]{0:T(128)S(1)} all-reduce(f32[64]{0:T(128)S(1)} %get-tuple-element.6), channel_id=5, replica_groups=mesh['dp'=4,'mp'=8] {'dp'}, use_global_device_ids=true, to_apply=%region_8.11.clone | all-reduce | flops 64 | bytes 512
  152.9 7.7 %reduce-scatter.5.cloned.1.call-done = f32[16,1280]{1,0:T(8,128)} async-done(((f32[64,1280]{1,0:T(8,128)}), f32[16,1280]{1,0:T(8,128)}) %reduce-scatter.5.cloned.1.call-update) | async-done | bytes 81936 | tf_op jit(solution)/shard_map/reduce_scatter | solution.py:96
  162.3 3.7 %all-to-all-start.2 = ((f32[8,2,1280]{2,1,0:T(2,128)}), f32[8,2,1280]{2,1,0:T(2,128)S(1)}, u32[]{:S(2)}, u32[]{:S(2)}) async-start(f32[8,2,1280]{2,1,0:T(2,128)} %all_to_all.59), calls=%async_computation.4 | async-start | bytes 163840 | tf_op jit(solution)/shard_map/all_to_all | solution.py:100
  166.7 4.3 %all-to-all-done.2 = f32[8,2,1280]{2,1,0:T(2,128)S(1)} async-done(((f32[8,2,1280]{2,1,0:T(2,128)}), f32[8,2,1280]{2,1,0:T(2,128)S(1)}, u32[]{:S(2)}, u32[]{:S(2)}) %all-to-all-start.2) | async-done | bytes 81952 | tf_op jit(solution)/shard_map/all_to_all | solution.py:100
  171.4 2.4 fusion.61
  174.2 2.0 fusion.12
  176.9 3.3 %all-to-all-start.3 = ((bf16[2,8,1024]{2,0,1:T(2,128)(2,1)}), bf16[2,8,1024]{2,0,1:T(2,128)(2,1)S(1)}, u32[]{:S(2)}, u32[]{:S(2)}) async-start(bf16[2,8,1024]{2,0,1:T(2,128)(2,1)} %copy.24), calls=%async_computation.5 | async-start | bytes 65536 | tf_op jit(solution)/shard_map/all_to_all | solution.py:122
  180.3 4.7 %all-to-all-done.3 = bf16[2,8,1024]{2,0,1:T(2,128)(2,1)S(1)} async-done(((bf16[2,8,1024]{2,0,1:T(2,128)(2,1)}), bf16[2,8,1024]{2,0,1:T(2,128)(2,1)S(1)}, u32[]{:S(2)}, u32[]{:S(2)}) %all-to-all-start.3) | async-done | bytes 32800 | tf_op jit(solution)/shard_map/all_to_all | solution.py:122
  185.1 13.5 %all_gather.7 = bf16[64,1024]{1,0:T(8,128)(2,1)S(1)} all-gather(bf16[16,1024]{1,0:T(8,128)(2,1)S(1)} %all_to_all.65), channel_id=1, replica_groups=mesh['dp'=4,'mp'=8] {'dp'}, dimensions={0}, use_global_device_ids=true | all-gather | bytes 163840 | tf_op jit(solution)/shard_map/all_gather | solution.py:124
  198.6 3.8 %fusion.63 = f32[64,2048]{1,0:T(8,128)} fusion(bf16[64,1024]{1,0:T(8,128)(2,1)S(1)} %all_gather.7, bf16[1024,2048]{1,0:T(8,128)(2,1)} %param.17), kind=kOutput, calls=%fused_computation.122 | convolution fusion | flops 268435456 | bytes 4849664 | tf_op jit(solution)/shard_map/dot_general | solution.py:123
  202.5 51.1 %all-reduce.7.cloned.1.call-done = f32[64,2048]{1,0:T(8,128)} async-done(((f32[64,2048]{1,0:T(8,128)}), f32[64,2048]{1,0:T(8,128)}) %all-reduce.7.cloned.1.call-update) | async-done | bytes 524304 | tf_op jit(solution)/shard_map/psum | solution.py:128
  (87 shorter events, 20.2 us)
Async XLA Ops:
  6.5 5.5 %copy-start = (bf16[2048,256]{1,0:T(8,128)(2,1)S(1)}, bf16[2048,256]{1,0:T(8,128)(2,1)}, u32[]{:S(2)}) copy-start(bf16[2048,256]{1,0:T(8,128)(2,1)} %param.16) | copy-start | bytes 3145732
  6.5 37.6 %reduce-scatter.3.cloned.1.call-start = ((), (), s32[]{:S(2)}) async-start(), calls=%async_computation.6 | async-start | bytes 409600 | tf_op jit(solution)/shard_map/reduce_scatter | solution.py:96
  16.5 19.3 %copy-start.1 = (s32[64]{0:T(128)S(1)}, s32[64]{0:T(128)}, u32[]{:S(2)}) copy-start(s32[64]{0:T(128)} %param.19) | copy-start | bytes 772
  16.5 20.1 %copy-start.2 = (u32[32]{0:T(128)S(1)}, u32[32]{0:T(128)}, u32[]{:S(2)}) copy-start(u32[32]{0:T(128)} %constant.56) | copy-start | bytes 388
  45.8 8.8 %all-to-all-start = ((f32[8,2,1280]{2,1,0:T(2,128)}), f32[8,2,1280]{2,1,0:T(2,128)S(1)}, u32[]{:S(2)}, u32[]{:S(2)}) async-start(f32[8,2,1280]{2,1,0:T(2,128)} %all_to_all.52), calls=%async_computation.1 | async-start | bytes 163840 | tf_op jit(solution)/shard_map/all_to_all | solution.py:100
  49.5 86.2 %all-reduce.5.cloned.1.call-start = ((), (), s32[]{:S(2)}) async-start(), calls=%async_computation.7 | async-start | bytes 1048576 | tf_op jit(solution)/shard_map/psum | solution.py:128
  84.5 76.1 %reduce-scatter.5.cloned.1.call-start = ((), (), s32[]{:S(2)}) async-start(), calls=%async_computation.8 | async-start | bytes 409600 | tf_op jit(solution)/shard_map/reduce_scatter | solution.py:96
  162.3 8.8 %all-to-all-start.2 = ((f32[8,2,1280]{2,1,0:T(2,128)}), f32[8,2,1280]{2,1,0:T(2,128)S(1)}, u32[]{:S(2)}, u32[]{:S(2)}) async-start(f32[8,2,1280]{2,1,0:T(2,128)} %all_to_all.59), calls=%async_computation.4 | async-start | bytes 163840 | tf_op jit(solution)/shard_map/all_to_all | solution.py:100
  176.9 8.1 %all-to-all-start.3 = ((bf16[2,8,1024]{2,0,1:T(2,128)(2,1)}), bf16[2,8,1024]{2,0,1:T(2,128)(2,1)S(1)}, u32[]{:S(2)}, u32[]{:S(2)}) async-start(bf16[2,8,1024]{2,0,1:T(2,128)(2,1)} %copy.24), calls=%async_computation.5 | async-start | bytes 65536 | tf_op jit(solution)/shard_map/all_to_all | solution.py:122
  180.3 73.2 %all-reduce.7.cloned.1.call-start = ((), (), s32[]{:S(2)}) async-start(), calls=%async_computation.9 | async-start | bytes 1048576 | tf_op jit(solution)/shard_map/psum | solution.py:128
Sparse Core Ops, SparseCore 0:
  16.4 22.8 reduce-scatter.2
  84.7 50.9 all-reduce.4
  141.2 19.3 reduce-scatter.4
  202.6 50.9 all-reduce.6
where the time goes:
time: 264 us; the launch traced here: 263 us
  waiting for transfers between devices  124 us (47%)
  blocking collectives  59.3 us (22%)
  matrix products  23.7 us (9%)
  local copies, waits for them, and re-layouts  20.5 us (8%)
  between operations  14.1 us (5%)
  starting transfers between devices  10.8 us (4%)
  other arithmetic  10.4 us (4%)
    psum x2, waiting for transfers between devices, shards(): totals = lax.psum(partial_out, 'mp')  102 us
    all_gather x2, blocking collectives, shards(): lax.all_gather(returned, 'dp', axis=0, tiled=True)  27 us
    unnamed x2, blocking collectives  25.1 us
    all_to_all x2, waiting for transfers between devices, shards(): lax.all_to_all(projected, 'mp', split_axis=0, concat_axis=1, tiled=True)  9.31 us
    reduce_scatter x2, waiting for transfers between devices, shards(): lax.psum_scatter(partial_value, 'dp', scatter_dimension=0, tiled=True)  7.74 us
    dot_general x2, matrix products, shards(): jnp.dot(lax.all_gather(returned, 'dp', axis=0, tiled=True), w_out, prefer...  7.69 us
    all_to_all x2, starting transfers between devices, shards(): lax.all_to_all(projected, 'mp', split_axis=0, concat_axis=1, tiled=True)  7.36 us
    all_to_all x1, blocking collectives, shards(): lax.all_to_all(attended, 'mp', split_axis=1, concat_axis=0, tiled=True)  7.22 us
  transfers between devices with their start and end apart: 7, of which 6 were waited for; matrix products, arithmetic and copies ran while one was open for 6% of the time, Pallas kernels for 0%

commit v1 on v0

--- a/solution.py
+++ b/solution.py
@@ -1,8 +1,11 @@
+import functools
 import math
 
 import jax
 import jax.numpy as jnp
 from jax import lax
+from jax.experimental import pallas as pl
+from jax.experimental.pallas import tpu as pltpu
 from jax.sharding import PartitionSpec as P
 
 LAYERS = 2
@@ -130,6 +133,479 @@
     return jnp.take(current, inverse, axis=0)
 
 
+LINK = jnp.bfloat16
+
+
+def fused_kernel(
+    sizes,
+    slot_s,
+    length_s,
+    slot_col,
+    slot_row,
+    cos_ref,
+    sin_ref,
+    hidden_ref,
+    gain_ref,
+    wq_hbm,
+    wkv_hbm,
+    wo_hbm,
+    cache_hbm,
+    out_ref,
+    wq,
+    wkv,
+    wo,
+    cache,
+    state,
+    scaled,
+    part_own,
+    square_send,
+    square_recv,
+    part_send,
+    part_recv,
+    proj_send,
+    proj_recv,
+    query_buf,
+    fresh_buf,
+    att_buf,
+    att_send,
+    att_recv,
+    att_rows,
+    gathered,
+    out_own,
+    out_send,
+    out_recv,
+    load_sem,
+    sq_ssem,
+    sq_rsem,
+    pa_ssem,
+    pa_rsem,
+    pr_ssem,
+    pr_rsem,
+    at_ssem,
+    at_rsem,
+    ga_ssem,
+    ga_rsem,
+    ou_ssem,
+    ou_rsem,
+    st_ssem,
+    st_rsem,
+):
+    n_dp, n_mp, rows, width, query_cols, keyval_cols, owned, key_heads, head_dim = sizes
+    band = rows // n_dp
+    chunk = width // n_mp
+    group = query_cols // head_dim
+    block = keyval_cols
+    blocks = (query_cols + keyval_cols) // block
+    d = lax.axis_index("dp")
+    m = lax.axis_index("mp")
+    model_width = width * n_dp
+    score_scale = 1.0 / math.sqrt(head_dim)
+
+    loads = [
+        pltpu.make_async_copy(wkv_hbm, wkv, load_sem.at[0]),
+        pltpu.make_async_copy(wq_hbm, wq, load_sem.at[1]),
+        pltpu.make_async_copy(cache_hbm.at[0], cache.at[0], load_sem.at[2]),
+    ]
+    for j in range(n_mp):
+        loads.append(
+            pltpu.make_async_copy(
+                wo_hbm.at[:, pl.ds(j * chunk, chunk)], wo.at[j], load_sem.at[3 + j]
+            )
+        )
+    for layer in range(1, LAYERS):
+        loads.append(
+            pltpu.make_async_copy(
+                cache_hbm.at[layer], cache.at[layer], load_sem.at[2 + n_mp + layer]
+            )
+        )
+    for one in loads:
+        one.start()
+
+    barrier = pltpu.get_barrier_semaphore()
+    for k in range(1, n_dp):
+        pl.semaphore_signal(
+            barrier,
+            inc=1,
+            device_id={"dp": lax.rem(d + k, n_dp)},
+            device_id_type=pl.DeviceIdType.MESH,
+        )
+    for k in range(1, n_mp):
+        pl.semaphore_signal(
+            barrier,
+            inc=1,
+            device_id={"mp": lax.rem(m + k, n_mp)},
+            device_id_type=pl.DeviceIdType.MESH,
+        )
+
+    lanes = lax.broadcasted_iota(jnp.int32, (rows, rows), 1)
+    pick = jnp.where(slot_col[...] == lanes, 1.0, 0.0).astype(jnp.bfloat16)
+    for c in range(n_mp):
+        state[0, c] = jnp.dot(
+            pick, hidden_ref[:, c * chunk : (c + 1) * chunk], preferred_element_type=jnp.float32
+        ).astype(jnp.bfloat16)
+
+    pl.semaphore_wait(barrier, n_dp - 1 + n_mp - 1)
+
+    sends = []
+
+    def remote(src, dst, ssem, rsem, where):
+        copy = pltpu.make_async_remote_copy(
+            src_ref=src,
+            dst_ref=dst,
+            send_sem=ssem,
+            recv_sem=rsem,
+            device_id=where,
+            device_id_type=pl.DeviceIdType.MESH,
+        )
+        copy.start()
+        sends.append(copy)
+        return copy
+
+    arriving = []
+    for layer in range(LAYERS):
+        for copy in arriving:
+            copy.wait_recv()
+        squares = jnp.zeros((rows, 128), jnp.float32)
+        for c in range(n_mp):
+            floats = state[layer, c].astype(jnp.float32)
+            gain = gain_ref[:, c * chunk : (c + 1) * chunk].astype(jnp.float32)
+            scaled[:, c * chunk : (c + 1) * chunk] = (floats * gain).astype(jnp.bfloat16)
+            for t in range(chunk // 128):
+                piece = floats[:, t * 128 : (t + 1) * 128]
+                squares = squares + piece * piece
+        square_row = jnp.sum(squares, axis=1, keepdims=True)
+        square_send[layer] = jnp.broadcast_to(square_row, (rows, 128)).reshape(n_dp, band, 128)
+        square_copies = []
+        for k in range(1, n_dp):
+            to = lax.rem(d + k, n_dp)
+            square_copies.append(
+                remote(
+                    square_send.at[layer, to],
+                    square_recv.at[layer, k - 1],
+                    sq_ssem.at[layer, k - 1],
+                    sq_rsem.at[layer, k - 1],
+                    {"dp": to},
+                )
+            )
+        part_copies = []
+        for b in range(blocks):
+            if b == 0:
+                if layer == 0:
+                    loads[0].wait()
+                weights = wkv[...]
+            else:
+                if layer == 0 and b == 1:
+                    loads[1].wait()
+                weights = wq[:, (b - 1) * block : b * block]
+            product = jnp.dot(scaled[...], weights, preferred_element_type=jnp.float32)
+            product = product.reshape(n_dp, band, block)
+            part_own[b] = product
+            part_send[layer, b] = product.astype(LINK)
+            for k in range(1, n_dp):
+                to = lax.rem(d + k, n_dp)
+                part_copies.append(
+                    remote(
+                        part_send.at[layer, b, to],
+                        part_recv.at[layer, b, k - 1],
+                        pa_ssem.at[layer, b, k - 1],
+                        pa_rsem.at[layer, b, k - 1],
+                        {"dp": to},
+                    )
+                )
+        for copy in square_copies:
+            copy.wait_recv()
+        square_sum = square_send[layer, d]
+        for k in range(1, n_dp):
+            square_sum = square_sum + square_recv[layer, k - 1]
+        inverse_rms = lax.rsqrt(square_sum / model_width + norm_eps)[:, :1]
+        for copy in part_copies:
+            copy.wait_recv()
+        for b in range(blocks):
+            total = part_own[b, d]
+            for k in range(1, n_dp):
+                total = total + part_recv[layer, b, k - 1].astype(jnp.float32)
+            total = total * inverse_rms
+            start = query_cols if b == 0 else (b - 1) * block
+            for j in range(n_mp):
+                proj_send[layer, j, :, start : start + block] = total[
+                    j * owned : (j + 1) * owned
+                ]
+        proj_copies = []
+        for k in range(1, n_mp):
+            to = lax.rem(m + k, n_mp)
+            proj_copies.append(
+                remote(
+                    proj_send.at[layer, to],
+                    proj_recv.at[layer, m],
+                    pr_ssem.at[layer, k - 1],
+                    pr_rsem.at[layer, k - 1],
+                    {"mp": to},
+                )
+            )
+        proj_recv[layer, m] = proj_send[layer, m]
+        for copy in proj_copies:
+            copy.wait_recv()
+
+        if layer == 0:
+            loads[2].wait()
+        else:
+            loads[2 + n_mp + layer].wait()
+        for r in range(owned):
+            slot = slot_s[(d * n_mp + m) * owned + r]
+            cosines = cos_ref[pl.ds(slot, 1), :]
+            sines = sin_ref[pl.ds(slot, 1), :]
+            length = length_s[slot]
+
+            def turned(x):
+                return x * cosines + pltpu.roll(x, head_dim // 2, 1) * sines
+
+            for g in range(group):
+                query_buf[r, :, g, :] = turned(
+                    proj_recv[layer, :, r, g * head_dim : (g + 1) * head_dim]
+                )
+            per = keyval_cols // head_dim
+            key_sources = key_heads // per
+            for t in range(per):
+                start = query_cols + t * head_dim
+                fresh = proj_recv[layer, :, r, start : start + head_dim]
+                keys_fresh = turned(fresh)
+                for source in range(n_mp):
+                    kind = source // key_sources
+                    head = (source % key_sources) * per + t
+                    row = keys_fresh if kind == 0 else fresh
+                    fresh_buf[r, kind, head : head + 1, :] = row[source : source + 1]
+            queries = query_buf[r].astype(jnp.bfloat16)
+            fresh_keys = fresh_buf[r, 0].astype(jnp.bfloat16).astype(jnp.float32)
+            fresh_values = fresh_buf[r, 1].astype(jnp.bfloat16).astype(jnp.float32)
+            key_rows = cache[layer, r, 0]
+            value_rows = cache[layer, r, 1]
+            scores = (
+                lax.dot_general(
+                    queries,
+                    key_rows,
+                    (((2,), (2,)), ((0,), (0,))),
+                    preferred_element_type=jnp.float32,
+                )
+                * score_scale
+            )
+            own_score = (
+                jnp.sum(
+                    queries.astype(jnp.float32) * fresh_keys[:, None, :], axis=2, keepdims=True
+                )
+                * score_scale
+            )
+            at = lax.broadcasted_iota(jnp.int32, scores.shape, 2)
+            scores = jnp.where(at < length, scores, -jnp.inf)
+            highest = jnp.maximum(jnp.max(scores, axis=2, keepdims=True), own_score)
+            weights = jnp.exp(scores - highest)
+            own_weight = jnp.exp(own_score - highest)
+            denominator = jnp.sum(weights, axis=2, keepdims=True) + own_weight
+            summed = lax.dot_general(
+                weights.astype(jnp.bfloat16),
+                value_rows,
+                (((2,), (1,)), ((0,), (0,))),
+                preferred_element_type=jnp.float32,
+            )
+            own_rounded = own_weight.astype(jnp.bfloat16).astype(jnp.float32)
+            summed = summed + own_rounded * fresh_values[:, None, :]
+            att_buf[r] = summed / denominator
+            for g in range(group):
+                att_send[layer, :, r, g * head_dim : (g + 1) * head_dim] = att_buf[r, :, g, :]
+        att_copies = []
+        for k in range(1, n_mp):
+            to = lax.rem(m + k, n_mp)
+            att_copies.append(
+                remote(
+                    att_send.at[layer, to],
+                    att_recv.at[layer, m],
+                    at_ssem.at[layer, k - 1],
+                    at_rsem.at[layer, k - 1],
+                    {"mp": to},
+                )
+            )
+        att_recv[layer, m] = att_send[layer, m]
+        for copy in att_copies:
+            copy.wait_recv()
+        for j in range(n_mp):
+            att_rows[j * owned : (j + 1) * owned, :] = att_recv[layer, j]
+        gathered[layer, d] = att_rows[...].astype(jnp.bfloat16)
+        gather_copies = []
+        for k in range(1, n_dp):
+            gather_copies.append(
+                remote(
+                    gathered.at[layer, d],
+                    gathered.at[layer, d],
+                    ga_ssem.at[layer, k - 1],
+                    ga_rsem.at[layer, k - 1],
+                    {"dp": lax.rem(d + k, n_dp)},
+                )
+            )
+        for copy in gather_copies:
+            copy.wait_recv()
+        if layer == 0:
+            for j in range(n_mp):
+                loads[3 + j].wait()
+        left = gathered[layer].reshape(rows, query_cols)
+        out_copies = []
+        for k in range(1, n_mp):
+            to = lax.rem(m + k, n_mp)
+            product = jnp.dot(left, wo[to], preferred_element_type=jnp.float32)
+            out_send[layer, k - 1] = product.astype(LINK)
+            out_copies.append(
+                remote(
+                    out_send.at[layer, k - 1],
+                    out_recv.at[layer, k - 1],
+                    ou_ssem.at[layer, k - 1],
+                    ou_rsem.at[layer, k - 1],
+                    {"mp": to},
+                )
+            )
+        out_own[...] = state[layer, m].astype(jnp.float32) + jnp.dot(
+            left, wo[m], preferred_element_type=jnp.float32
+        )
+        for copy in out_copies:
+            copy.wait_recv()
+        total = out_own[...]
+        for k in range(1, n_mp):
+            total = total + out_recv[layer, k - 1].astype(jnp.float32)
+        state[layer + 1, m] = total.astype(jnp.bfloat16)
+        arriving = []
+        for k in range(1, n_mp):
+            arriving.append(
+                remote(
+                    state.at[layer + 1, m],
+                    state.at[layer + 1, m],
+                    st_ssem.at[layer, k - 1],
+                    st_rsem.at[layer, k - 1],
+                    {"mp": lax.rem(m + k, n_mp)},
+                )
+            )
+    for copy in arriving:
+        copy.wait_recv()
+    sublanes = lax.broadcasted_iota(jnp.int32, (rows, rows), 0)
+    place = jnp.where(slot_row[...] == sublanes, 1.0, 0.0).astype(jnp.bfloat16)
+    for c in range(n_mp):
+        out_ref[:, c * chunk : (c + 1) * chunk] = jnp.dot(
+            place, state[LAYERS, c], preferred_element_type=jnp.float32
+        ).astype(jnp.bfloat16)
+    for copy in sends:
+        copy.wait_send()
+
+
+def fused(
+    hidden_in, norm_gain, w_query, w_keyval, w_out, cache_slots, lengths, positions, slot_order
+):
+    n_dp = lax.axis_size("dp")
+    n_mp = lax.axis_size("mp")
+    rows, width = hidden_in.shape
+    query_cols = w_query.shape[1]
+    keyval_cols = w_keyval.shape[1]
+    owned, key_heads, cache_rows, head_dim = (
+        cache_slots.shape[1],
+        cache_slots.shape[3],
+        cache_slots.shape[4],
+        cache_slots.shape[5],
+    )
+    group = query_cols // head_dim
+    band = rows // n_dp
+    chunk = width // n_mp
+    blocks = (query_cols + keyval_cols) // keyval_cols
+    half_dim = head_dim // 2
+    index_row = jnp.arange(half_dim, dtype=jnp.float32)
+    frequency = jnp.exp(index_row * (-2.0 * math.log(rope_base) / head_dim))
+    angles = positions.astype(jnp.float32)[:, None] * jnp.concatenate([frequency, frequency])
+    sign = jnp.where(jnp.arange(head_dim) < half_dim, -1.0, 1.0)
+    cosines = jnp.cos(angles)
+    sines = jnp.sin(angles) * sign
+    sizes = (n_dp, n_mp, rows, width, query_cols, keyval_cols, owned, key_heads, head_dim)
+    vmem = pl.BlockSpec(memory_space=pltpu.VMEM)
+    smem = pl.BlockSpec(memory_space=pltpu.SMEM)
+    anywhere = pl.BlockSpec(memory_space=pl.ANY)
+    f32, bf16 = jnp.float32, jnp.bfloat16
+    dma = pltpu.SemaphoreType.DMA
+    return pl.pallas_call(
+        functools.partial(fused_kernel, sizes),
+        out_shape=jax.ShapeDtypeStruct((rows, width), bf16),
+        in_specs=[smem, smem, vmem, vmem, vmem, vmem, vmem, vmem] + [anywhere] * 4,
+        out_specs=vmem,
+        scratch_shapes=[
+            pltpu.VMEM(w_query.shape, bf16),
+            pltpu.VMEM(w_keyval.shape, bf16),
+            pltpu.VMEM((n_mp, query_cols, chunk), bf16),
+            pltpu.VMEM(cache_slots.shape, bf16),
+            pltpu.VMEM((LAYERS + 1, n_mp, rows, chunk), bf16),
+            pltpu.VMEM((rows, width), bf16),
+            pltpu.VMEM((blocks, n_dp, band, keyval_cols), f32),
+            pltpu.VMEM((LAYERS, n_dp, band, 128), f32),
+            pltpu.VMEM((LAYERS, n_dp - 1, band, 128), f32),
+            pltpu.VMEM((LAYERS, blocks, n_dp, band, keyval_cols), LINK),
+            pltpu.VMEM((LAYERS, blocks, n_dp - 1, band, keyval_cols), LINK),
+            pltpu.VMEM((LAYERS, n_mp, owned, query_cols + keyval_cols), f32),
+            pltpu.VMEM((LAYERS, n_mp, owned, query_cols + keyval_cols), f32),
+            pltpu.VMEM((owned, n_mp, group, head_dim), f32),
+            pltpu.VMEM((owned, 2, key_heads, head_dim), f32),
+            pltpu.VMEM((owned, n_mp, group, head_dim), f32),
+            pltpu.VMEM((LAYERS, n_mp, owned, query_cols), f32),
+            pltpu.VMEM((LAYERS, n_mp, owned, query_cols), f32),
+            pltpu.VMEM((band, query_cols), f32),
+            pltpu.VMEM((LAYERS, n_dp, band, query_cols), bf16),
+            pltpu.VMEM((rows, chunk), f32),
+            pltpu.VMEM((LAYERS, n_mp - 1, rows, chunk), LINK),
+            pltpu.VMEM((LAYERS, n_mp - 1, rows, chunk), LINK),
+            dma((2 + n_mp + LAYERS,)),
+            dma((LAYERS, n_dp - 1)),
+            dma((LAYERS, n_dp - 1)),
+            dma((LAYERS, blocks, n_dp - 1)),
+            dma((LAYERS, blocks, n_dp - 1)),
+            dma((LAYERS, n_mp - 1)),
+            dma((LAYERS, n_mp - 1)),
+            dma((LAYERS, n_mp - 1)),
+            dma((LAYERS, n_mp - 1)),
+            dma((LAYERS, n_dp - 1)),
+            dma((LAYERS, n_dp - 1)),
+            dma((LAYERS, n_mp - 1)),
+            dma((LAYERS, n_mp - 1)),
+            dma((LAYERS, n_mp - 1)),
+            dma((LAYERS, n_mp - 1)),
+        ],
+        compiler_params=pltpu.CompilerParams(
+            collective_id=0, has_side_effects=True, vmem_limit_bytes=56 << 20
+        ),
+    )(
+        slot_order,
+        lengths,
+        slot_order.reshape(rows, 1),
+        slot_order.reshape(1, rows),
+        cosines,
+        sines,
+        hidden_in,
+        norm_gain.reshape(1, width),
+        w_query,
+        w_keyval,
+        w_out,
+        cache_slots,
+    )
+
+
+def dispatch(
+    hidden_in, norm_gain, w_query, w_keyval, w_out, cache_slots, lengths, positions, slot_order
+):
+    n_mp = lax.axis_size("mp")
+    key_heads = cache_slots.shape[3]
+    head_dim = cache_slots.shape[5]
+    fits = (
+        key_heads == n_mp
+        and w_keyval.shape[1] % head_dim == 0
+        and w_query.shape[1] % w_keyval.shape[1] == 0
+        and hidden_in.shape[1] % (128 * n_mp) == 0
+        and hidden_in.shape[0] % (16 * lax.axis_size("dp")) == 0
+    )
+    chosen = fused if fits else shards
+    return chosen(
+        hidden_in, norm_gain, w_query, w_keyval, w_out, cache_slots, lengths, positions, slot_order
+    )
+
+
 def solution(mesh):
     placed = (
         P(None, "dp"),
@@ -143,5 +619,5 @@
         P(),
     )
     return jax.shard_map(
-        shards, mesh=mesh, in_specs=placed, out_specs=P(None, "dp"), check_vma=False
-    )
+        dispatch, mesh=mesh, in_specs=placed, out_specs=P(None, "dp"), check_vma=False
+    )

time: 264 us -> 72.2 us (0.27)
  waiting for transfers between devices: 124 us -> 0 us
  Pallas kernels: 0 us -> 66 us
  blocking collectives: 59.3 us -> 0 us
  matrix products: 23.7 us -> 0 us
  local copies, waits for them, and re-layouts: 20.5 us -> 4.32 us
  between operations: 14.1 us -> 0.01 us
  starting transfers between devices: 10.8 us -> 0 us
  other arithmetic: 10.4 us -> 1.57 us
    psum x2 -> x0, waiting for transfers between devices: 102 us -> none  [shards(): totals = lax.psum(partial_out, 'mp')]
    pallas_call x0 -> x1, Pallas kernels: none -> 66 us  [fused(): pl.pallas_call(functools.partial(fused_kernel, sizes), out_shape=jax.Shap...]
    all_gather x2 -> x0, blocking collectives: 27 us -> none  [shards(): lax.all_gather(returned, 'dp', axis=0, tiled=True)]
    unnamed x2 -> x0, blocking collectives: 25.1 us -> none
    dot_general x12 -> x0, matrix products: 23.7 us -> none  [the longest x2 7.69 us: shards(): jnp.dot(lax.all_gather(returned, 'dp', axis=0, tiled=True), w_out, prefer...]
    all_to_all x3 -> x0, waiting for transfers between devices: 14 us -> none  [the longest x2 9.31 us: shards(): lax.all_to_all(projected, 'mp', split_axis=0, concat_axis=1, tiled=True)]
    all_to_all x3 -> x0, starting transfers between devices: 10.7 us -> none  [the longest x2 7.36 us: shards(): lax.all_to_all(projected, 'mp', split_axis=0, concat_axis=1, tiled=True)]
    reduce_scatter x2 -> x0, waiting for transfers between devices: 7.74 us -> none  [shards(): lax.psum_scatter(partial_value, 'dp', scatter_dimension=0, tiled=True)]
  transfers between devices with their start and end apart: 7 -> 0, of which waited for: 6 -> 0; matrix products, arithmetic and copies ran while one was open for 6% -> 0% of each run, Pallas kernels for 0% -> 0%
where the time goes in v1:
time: 72.2 us; the launch traced here: 71.9 us
  Pallas kernels  66 us (91%)
  local copies, waits for them, and re-layouts  4.32 us (6%)
  other arithmetic  1.57 us (2%)
    pallas_call x1, Pallas kernels, fused(): pl.pallas_call(functools.partial(fused_kernel, sizes), out_shape=jax.Shap...  66 us
    unnamed x1, local copies, waits for them, and re-layouts  1.67 us

profile of v1, /device:TPU:0, one launch (start us, length us, event | category | flops | bytes accessed | tf_op | source)
XLA Modules:
  0.0 71.9 jit_solution(9624863290138426155)
XLA Ops:
  0.0 0.7 convert_element_type.3
  0.7 0.1 compare_select_fusion
  0.7 1.3 %reshape.18.gain_ref = bf16[1,2048]{1,0:T(2,128)(2,1)} reshape(bf16[2048]{0:T(1024)(128)(2,1)} %param.10) | data formatting | bytes 8192 | tf_op jit(solution)/shard_map/reshape | solution.py:582
  2.0 1.4 %copy.10.slot_col = s32[64,1]{1,0:T(8,128)} copy(s32[64,1]{0,1:T(1,128)} %bitcast.2) | data formatting | bytes 512 | tf_op jit(solution)/shard_map/reshape | solution.py:577
  3.4 0.8 %fusion = (f32[64,128]{1,0:T(8,128)}, f32[64,128]{1,0:T(8,128)}) fusion(f32[128]{0:T(128)S(1)} %get-tuple-element.7, f32[128]{0:T(128)S(1)} %get-tuple-element.8, f32[64]{0:T(128)S(1)} %convert_element_type.3), kind=kLoop, calls=%fused_computation.2 | loop fusion | flops 16384 | bytes 66816 | tf_op jit(solution)/shard_map/mul | solution.py:519
  4.2 66.0 %shard_map.91 = bf16[64,2048]{1,0:T(8,128)(2,1)} custom-call(s32[64]{0:T(128)} %slot_s.1, s32[64]{0:T(128)} %length_s.1, s32[64,1]{1,0:T(8,128)} %copy.10.slot_col, s32[1,64]{1,0:T(1,128)} %bitcast.3, f32[64,128]{1,0:T(8,128)} %get-tuple-element.6.cos_ref, f32[64,128]{1,0:T(8,128)} %get-tuple-element.5.sin_ref, bf16[64,2048]{1,0:T(8,128)(2,1)} %hidden_ref.1, ...), custom_call_target="tpu_custom_call" | custom-call | tf_op jit(solution)/shard_map/pallas_call | solution.py:526
  70.3 1.7 %copy.12 = bf16[64,2048]{1,0:T(8,128)(2,1)} copy(bf16[64,2048]{1,0:T(8,128)(2,1)} %shard_map.91) | data formatting | bytes 524288
  (1 shorter events, 0.0 us)

commit v2 on v1

--- a/solution.py
+++ b/solution.py
@@ -3,6 +3,7 @@
 
 import jax
 import jax.numpy as jnp
+import numpy as np
 from jax import lax
 from jax.experimental import pallas as pl
 from jax.experimental.pallas import tpu as pltpu
@@ -140,10 +141,9 @@
     sizes,
     slot_s,
     length_s,
-    slot_col,
+    position_s,
     slot_row,
-    cos_ref,
-    sin_ref,
+    frequency_ref,
     hidden_ref,
     gain_ref,
     wq_hbm,
@@ -171,9 +171,9 @@
     att_recv,
     att_rows,
     gathered,
-    out_own,
-    out_send,
-    out_recv,
+    pair_send,
+    pair_recv,
+    out_all,
     load_sem,
     sq_ssem,
     sq_rsem,
@@ -185,6 +185,8 @@
     at_rsem,
     ga_ssem,
     ga_rsem,
+    pq_ssem,
+    pq_rsem,
     ou_ssem,
     ou_rsem,
     st_ssem,
@@ -199,6 +201,11 @@
     d = lax.axis_index("dp")
     m = lax.axis_index("mp")
     model_width = width * n_dp
+    core = lax.rem(m, 2)
+    chip = m // 2
+    sibling = m + 1 - 2 * core
+    n_chip = n_mp // 2
+    half = n_mp // 2
     score_scale = 1.0 / math.sqrt(head_dim)
 
     loads = [
@@ -237,14 +244,29 @@
             device_id_type=pl.DeviceIdType.MESH,
         )
 
-    lanes = lax.broadcasted_iota(jnp.int32, (rows, rows), 1)
-    pick = jnp.where(slot_col[...] == lanes, 1.0, 0.0).astype(jnp.bfloat16)
+    sublanes = lax.broadcasted_iota(jnp.int32, (rows, rows), 0)
+    place = jnp.where(slot_row[...] == sublanes, 1.0, 0.0).astype(jnp.bfloat16)
+    gains = gain_ref[...].astype(jnp.float32)
     for c in range(n_mp):
-        state[0, c] = jnp.dot(
-            pick, hidden_ref[:, c * chunk : (c + 1) * chunk], preferred_element_type=jnp.float32
+        state[0, c] = lax.dot_general(
+            place,
+            hidden_ref[:, c * chunk : (c + 1) * chunk],
+            (((0,), (0,)), ((), ())),
+            preferred_element_type=jnp.float32,
         ).astype(jnp.bfloat16)
 
     pl.semaphore_wait(barrier, n_dp - 1 + n_mp - 1)
+
+    turns = []
+    for r in range(owned):
+        slot = slot_s[(d * n_mp + m) * owned + r]
+        at = jnp.full((8, head_dim), position_s[slot], jnp.int32).astype(jnp.float32)
+        angles = at * frequency_ref[...]
+        lane = lax.broadcasted_iota(jnp.int32, (8, head_dim), 1)
+        sines = jnp.sin(angles)
+        turns.append(
+            (jnp.cos(angles), jnp.where(lane < head_dim // 2, -sines, sines), length_s[slot])
+        )
 
     sends = []
 
@@ -268,10 +290,12 @@
         squares = jnp.zeros((rows, 128), jnp.float32)
         for c in range(n_mp):
             floats = state[layer, c].astype(jnp.float32)
-            gain = gain_ref[:, c * chunk : (c + 1) * chunk].astype(jnp.float32)
-            scaled[:, c * chunk : (c + 1) * chunk] = (floats * gain).astype(jnp.bfloat16)
             for t in range(chunk // 128):
                 piece = floats[:, t * 128 : (t + 1) * 128]
+                at = c * (chunk // 128) + t
+                scaled[:, at * 128 : (at + 1) * 128] = (piece * gains[at : at + 1]).astype(
+                    jnp.bfloat16
+                )
                 squares = squares + piece * piece
         square_row = jnp.sum(squares, axis=1, keepdims=True)
         square_send[layer] = jnp.broadcast_to(square_row, (rows, 128)).reshape(n_dp, band, 128)
@@ -351,10 +375,7 @@
         else:
             loads[2 + n_mp + layer].wait()
         for r in range(owned):
-            slot = slot_s[(d * n_mp + m) * owned + r]
-            cosines = cos_ref[pl.ds(slot, 1), :]
-            sines = sin_ref[pl.ds(slot, 1), :]
-            length = length_s[slot]
+            cosines, sines, length = turns[r]
 
             def turned(x):
                 return x * cosines + pltpu.roll(x, head_dim // 2, 1) * sines
@@ -446,44 +467,55 @@
             for j in range(n_mp):
                 loads[3 + j].wait()
         left = gathered[layer].reshape(rows, query_cols)
+        pair_copies = []
+        for q in range(half):
+            pair_send[layer, q] = jnp.dot(
+                left, wo[(1 - core) * half + q], preferred_element_type=jnp.float32
+            )
+            pair_copies.append(
+                remote(
+                    pair_send.at[layer, q],
+                    pair_recv.at[layer, q],
+                    pq_ssem.at[layer, q],
+                    pq_rsem.at[layer, q],
+                    {"mp": sibling},
+                )
+            )
         out_copies = []
-        for k in range(1, n_mp):
-            to = lax.rem(m + k, n_mp)
-            product = jnp.dot(left, wo[to], preferred_element_type=jnp.float32)
-            out_send[layer, k - 1] = product.astype(LINK)
-            out_copies.append(
-                remote(
-                    out_send.at[layer, k - 1],
-                    out_recv.at[layer, k - 1],
-                    ou_ssem.at[layer, k - 1],
-                    ou_rsem.at[layer, k - 1],
-                    {"mp": to},
-                )
-            )
-        out_own[...] = state[layer, m].astype(jnp.float32) + jnp.dot(
-            left, wo[m], preferred_element_type=jnp.float32
-        )
-        for copy in out_copies:
-            copy.wait_recv()
-        total = out_own[...]
-        for k in range(1, n_mp):
-            total = total + out_recv[layer, k - 1].astype(jnp.float32)
-        state[layer + 1, m] = total.astype(jnp.bfloat16)
+        for q in range(half):
+            product = jnp.dot(left, wo[core * half + q], preferred_element_type=jnp.float32)
+            pair_copies[q].wait_recv()
+            out_all[layer, chip, q] = (product + pair_recv[layer, q]).astype(LINK)
+            for k in range(1, n_chip):
+                out_copies.append(
+                    remote(
+                        out_all.at[layer, chip, q],
+                        out_all.at[layer, chip, q],
+                        ou_ssem.at[layer, q, k - 1],
+                        ou_rsem.at[layer, q, k - 1],
+                        {"mp": lax.rem(chip + k, n_chip) * 2 + core},
+                    )
+                )
         arriving = []
-        for k in range(1, n_mp):
+        for q in range(half):
+            at = core * half + q
+            total = state[layer, at].astype(jnp.float32)
+            for k in range(1, n_chip):
+                out_copies[q * (n_chip - 1) + k - 1].wait_recv()
+            for c in range(n_chip):
+                total = total + out_all[layer, c, q].astype(jnp.float32)
+            state[layer + 1, at] = total.astype(jnp.bfloat16)
             arriving.append(
                 remote(
-                    state.at[layer + 1, m],
-                    state.at[layer + 1, m],
-                    st_ssem.at[layer, k - 1],
-                    st_rsem.at[layer, k - 1],
-                    {"mp": lax.rem(m + k, n_mp)},
+                    state.at[layer + 1, at],
+                    state.at[layer + 1, at],
+                    st_ssem.at[layer, q],
+                    st_rsem.at[layer, q],
+                    {"mp": sibling},
                 )
             )
     for copy in arriving:
         copy.wait_recv()
-    sublanes = lax.broadcasted_iota(jnp.int32, (rows, rows), 0)
-    place = jnp.where(slot_row[...] == sublanes, 1.0, 0.0).astype(jnp.bfloat16)
     for c in range(n_mp):
         out_ref[:, c * chunk : (c + 1) * chunk] = jnp.dot(
             place, state[LAYERS, c], preferred_element_type=jnp.float32
@@ -510,13 +542,9 @@
     band = rows // n_dp
     chunk = width // n_mp
     blocks = (query_cols + keyval_cols) // keyval_cols
-    half_dim = head_dim // 2
-    index_row = jnp.arange(half_dim, dtype=jnp.float32)
-    frequency = jnp.exp(index_row * (-2.0 * math.log(rope_base) / head_dim))
-    angles = positions.astype(jnp.float32)[:, None] * jnp.concatenate([frequency, frequency])
-    sign = jnp.where(jnp.arange(head_dim) < half_dim, -1.0, 1.0)
-    cosines = jnp.cos(angles)
-    sines = jnp.sin(angles) * sign
+    index_row = np.arange(head_dim) % (head_dim // 2)
+    frequency = np.exp(index_row * (-2.0 * math.log(rope_base) / head_dim))
+    frequency = jnp.asarray(frequency[None].astype(np.float32))
     sizes = (n_dp, n_mp, rows, width, query_cols, keyval_cols, owned, key_heads, head_dim)
     vmem = pl.BlockSpec(memory_space=pltpu.VMEM)
     smem = pl.BlockSpec(memory_space=pltpu.SMEM)
@@ -526,7 +554,7 @@
     return pl.pallas_call(
         functools.partial(fused_kernel, sizes),
         out_shape=jax.ShapeDtypeStruct((rows, width), bf16),
-        in_specs=[smem, smem, vmem, vmem, vmem, vmem, vmem, vmem] + [anywhere] * 4,
+        in_specs=[smem, smem, smem, vmem, vmem, vmem, vmem] + [anywhere] * 4,
         out_specs=vmem,
         scratch_shapes=[
             pltpu.VMEM(w_query.shape, bf16),
@@ -549,9 +577,9 @@
             pltpu.VMEM((LAYERS, n_mp, owned, query_cols), f32),
             pltpu.VMEM((band, query_cols), f32),
             pltpu.VMEM((LAYERS, n_dp, band, query_cols), bf16),
-            pltpu.VMEM((rows, chunk), f32),
-            pltpu.VMEM((LAYERS, n_mp - 1, rows, chunk), LINK),
-            pltpu.VMEM((LAYERS, n_mp - 1, rows, chunk), LINK),
+            pltpu.VMEM((LAYERS, n_mp // 2, rows, chunk), f32),
+            pltpu.VMEM((LAYERS, n_mp // 2, rows, chunk), f32),
+            pltpu.VMEM((LAYERS, n_mp // 2, n_mp // 2, rows, chunk), LINK),
             dma((2 + n_mp + LAYERS,)),
             dma((LAYERS, n_dp - 1)),
             dma((LAYERS, n_dp - 1)),
@@ -563,10 +591,12 @@
             dma((LAYERS, n_mp - 1)),
             dma((LAYERS, n_dp - 1)),
             dma((LAYERS, n_dp - 1)),
-            dma((LAYERS, n_mp - 1)),
-            dma((LAYERS, n_mp - 1)),
-            dma((LAYERS, n_mp - 1)),
-            dma((LAYERS, n_mp - 1)),
+            dma((LAYERS, n_mp // 2)),
+            dma((LAYERS, n_mp // 2)),
+            dma((LAYERS, n_mp // 2, n_mp // 2 - 1)),
+            dma((LAYERS, n_mp // 2, n_mp // 2 - 1)),
+            dma((LAYERS, n_mp // 2)),
+            dma((LAYERS, n_mp // 2)),
         ],
         compiler_params=pltpu.CompilerParams(
             collective_id=0, has_side_effects=True, vmem_limit_bytes=56 << 20
@@ -574,12 +604,11 @@
     )(
         slot_order,
         lengths,
-        slot_order.reshape(rows, 1),
+        positions,
         slot_order.reshape(1, rows),
-        cosines,
-        sines,
+        frequency,
         hidden_in,
-        norm_gain.reshape(1, width),
+        norm_gain.reshape(width // 128, 128),
         w_query,
         w_keyval,
         w_out,
@@ -595,6 +624,7 @@
     head_dim = cache_slots.shape[5]
     fits = (
         key_heads == n_mp
+        and n_mp % 2 == 0
         and w_keyval.shape[1] % head_dim == 0
         and w_query.shape[1] % w_keyval.shape[1] == 0
         and hidden_in.shape[1] % (128 * n_mp) == 0

time: 72.2 us -> 69.7 us (0.965)
  local copies, waits for them, and re-layouts: 4.32 us -> 1.67 us
  Pallas kernels: 66 us -> 67.6 us
  other arithmetic: 1.57 us -> 0 us
    reshape x2 -> x0, local copies, waits for them, and re-layouts: 2.65 us -> none  [the longest x1 1.36 us: fused(): slot_order.reshape(rows, 1)]
    pallas_call x1, Pallas kernels: 66 us -> 67.6 us  [fused(): pl.pallas_call(functools.partial(fused_kernel, sizes), out_shape=jax.Shap...]
    mul x1 -> x0, other arithmetic: 0.83 us -> none  [fused(): sines = jnp.sin(angles) * sign]
where the time goes in v2:
time: 69.7 us; the launch traced here: 69.3 us
  Pallas kernels  67.6 us (97%)
  local copies, waits for them, and re-layouts  1.67 us (2%)
    pallas_call x1, Pallas kernels, fused(): pl.pallas_call(functools.partial(fused_kernel, sizes), out_shape=jax.Shap...  67.6 us
    unnamed x1, local copies, waits for them, and re-layouts  1.67 us

profile of v2, /device:TPU:0, one launch (start us, length us, event | category | flops | bytes accessed | tf_op | source)
XLA Modules:
  0.0 69.3 jit_solution(14734432427540612503)
XLA Ops:
  0.0 67.6 %shard_map.100 = bf16[64,2048]{1,0:T(8,128)(2,1)} custom-call(s32[64]{0:T(128)} %slot_s.1, s32[64]{0:T(128)} %length_s.1, s32[64]{0:T(128)} %position_s.1, s32[1,64]{1,0:T(1,128)} %bitcast.3, f32[1,128]{1,0:T(1,128)} %constant.2.clone.frequency_ref, bf16[64,2048]{1,0:T(8,128)(2,1)} %hidden_ref.1, bf16[16,128]{1,0:T(8,128)(2,1)} %bitcast.2, ...), custom_call_target="tpu_custom_call" | custom-call | tf_op jit(solution)/shard_map/pallas_call | solution.py:554
  67.6 1.7 %copy.12 = bf16[64,2048]{1,0:T(8,128)(2,1)} copy(bf16[64,2048]{1,0:T(8,128)(2,1)} %shard_map.100) | data formatting | bytes 524288

commit v3 on v2

--- a/solution.py
+++ b/solution.py
@@ -168,7 +168,8 @@
     fresh_buf,
     att_buf,
     att_send,
-    att_recv,
+    att_pair,
+    att_quad,
     att_rows,
     gathered,
     pair_send,
@@ -181,8 +182,8 @@
     pa_rsem,
     pr_ssem,
     pr_rsem,
-    at_ssem,
-    at_rsem,
+    as_ssem,
+    as_rsem,
     ga_ssem,
     ga_rsem,
     pq_ssem,
@@ -229,19 +230,16 @@
         one.start()
 
     barrier = pltpu.get_barrier_semaphore()
-    for k in range(1, n_dp):
+    peers = [
+        {"dp": lax.rem(d + kd, n_dp), "mp": lax.rem(chip + kc, n_chip) * 2 + core}
+        for kd in range(n_dp)
+        for kc in range(n_chip)
+        if kd or kc
+    ]
+    peers += [{"mp": lax.rem(chip + kc, n_chip) * 2 + 1 - core} for kc in range(n_chip)]
+    for peer in peers:
         pl.semaphore_signal(
-            barrier,
-            inc=1,
-            device_id={"dp": lax.rem(d + k, n_dp)},
-            device_id_type=pl.DeviceIdType.MESH,
-        )
-    for k in range(1, n_mp):
-        pl.semaphore_signal(
-            barrier,
-            inc=1,
-            device_id={"mp": lax.rem(m + k, n_mp)},
-            device_id_type=pl.DeviceIdType.MESH,
+            barrier, inc=1, device_id=peer, device_id_type=pl.DeviceIdType.MESH
         )
 
     sublanes = lax.broadcasted_iota(jnp.int32, (rows, rows), 0)
@@ -255,8 +253,6 @@
             preferred_element_type=jnp.float32,
         ).astype(jnp.bfloat16)
 
-    pl.semaphore_wait(barrier, n_dp - 1 + n_mp - 1)
-
     turns = []
     for r in range(owned):
         slot = slot_s[(d * n_mp + m) * owned + r]
@@ -267,6 +263,8 @@
         turns.append(
             (jnp.cos(angles), jnp.where(lane < head_dim // 2, -sines, sines), length_s[slot])
         )
+
+    pl.semaphore_wait(barrier, n_chip + n_dp * n_chip - 1)
 
     sends = []
 
@@ -429,44 +427,50 @@
             )
             own_rounded = own_weight.astype(jnp.bfloat16).astype(jnp.float32)
             summed = summed + own_rounded * fresh_values[:, None, :]
-            att_buf[r] = summed / denominator
+            att_buf[r] = (summed / denominator).reshape(n_chip, 2, group, head_dim)
             for g in range(group):
-                att_send[layer, :, r, g * head_dim : (g + 1) * head_dim] = att_buf[r, :, g, :]
-        att_copies = []
-        for k in range(1, n_mp):
-            to = lax.rem(m + k, n_mp)
-            att_copies.append(
-                remote(
-                    att_send.at[layer, to],
-                    att_recv.at[layer, m],
-                    at_ssem.at[layer, k - 1],
-                    at_rsem.at[layer, k - 1],
-                    {"mp": to},
-                )
-            )
-        att_recv[layer, m] = att_send[layer, m]
-        for copy in att_copies:
-            copy.wait_recv()
-        for j in range(n_mp):
-            att_rows[j * owned : (j + 1) * owned, :] = att_recv[layer, j]
-        gathered[layer, d] = att_rows[...].astype(jnp.bfloat16)
+                for e in range(2):
+                    att_send[layer, e, :, r, g * head_dim : (g + 1) * head_dim] = att_buf[
+                        r, :, e, g, :
+                    ]
+        pair = remote(
+            att_send.at[layer, 1 - core],
+            att_pair.at[layer],
+            as_ssem.at[layer],
+            as_rsem.at[layer],
+            {"mp": sibling},
+        )
+        pair.wait_recv()
         gather_copies = []
-        for k in range(1, n_dp):
-            gather_copies.append(
-                remote(
-                    gathered.at[layer, d],
-                    gathered.at[layer, d],
-                    ga_ssem.at[layer, k - 1],
-                    ga_rsem.at[layer, k - 1],
-                    {"dp": lax.rem(d + k, n_dp)},
-                )
-            )
+        for kc in list(range(1, n_chip)) + [0]:
+            to_chip = lax.rem(chip + kc, n_chip)
+            mine = att_send[layer, core, to_chip]
+            other = att_pair[layer, to_chip]
+            att_quad[layer, kc, 0] = jnp.where(core == 0, mine, other).astype(jnp.bfloat16)
+            att_quad[layer, kc, 1] = jnp.where(core == 0, other, mine).astype(jnp.bfloat16)
+            for kd in range(n_dp):
+                if kc or kd:
+                    gather_copies.append(
+                        remote(
+                            att_quad.at[layer, kc],
+                            gathered.at[layer, d, chip],
+                            ga_ssem.at[layer, kc, kd],
+                            ga_rsem.at[layer, kc, kd],
+                            {"dp": lax.rem(d + kd, n_dp), "mp": to_chip * 2 + core},
+                        )
+                    )
+        gathered[layer, d, chip] = att_quad[layer, 0]
         for copy in gather_copies:
             copy.wait_recv()
+        for i in range(n_dp):
+            for c in range(n_chip):
+                for e in range(2):
+                    at = ((i * n_chip + c) * 2 + e) * owned
+                    att_rows[at : at + owned, :] = gathered[layer, i, c, e].astype(jnp.float32)
         if layer == 0:
             for j in range(n_mp):
                 loads[3 + j].wait()
-        left = gathered[layer].reshape(rows, query_cols)
+        left = att_rows[...].astype(jnp.bfloat16)
         pair_copies = []
         for q in range(half):
             pair_send[layer, q] = jnp.dot(
@@ -572,11 +576,12 @@
             pltpu.VMEM((LAYERS, n_mp, owned, query_cols + keyval_cols), f32),
             pltpu.VMEM((owned, n_mp, group, head_dim), f32),
             pltpu.VMEM((owned, 2, key_heads, head_dim), f32),
-            pltpu.VMEM((owned, n_mp, group, head_dim), f32),
-            pltpu.VMEM((LAYERS, n_mp, owned, query_cols), f32),
-            pltpu.VMEM((LAYERS, n_mp, owned, query_cols), f32),
-            pltpu.VMEM((band, query_cols), f32),
-            pltpu.VMEM((LAYERS, n_dp, band, query_cols), bf16),
+            pltpu.VMEM((owned, n_mp // 2, 2, group, head_dim), f32),
+            pltpu.VMEM((LAYERS, 2, n_mp // 2, owned, query_cols), f32),
+            pltpu.VMEM((LAYERS, n_mp // 2, owned, query_cols), f32),
+            pltpu.VMEM((LAYERS, n_mp // 2, 2, owned, query_cols), bf16),
+            pltpu.VMEM((rows, query_cols), f32),
+            pltpu.VMEM((LAYERS, n_dp, n_mp // 2, 2, owned, query_cols), bf16),
             pltpu.VMEM((LAYERS, n_mp // 2, rows, chunk), f32),
             pltpu.VMEM((LAYERS, n_mp // 2, rows, chunk), f32),
             pltpu.VMEM((LAYERS, n_mp // 2, n_mp // 2, rows, chunk), LINK),
@@ -587,10 +592,10 @@
             dma((LAYERS, blocks, n_dp - 1)),
             dma((LAYERS, n_mp - 1)),
             dma((LAYERS, n_mp - 1)),
-            dma((LAYERS, n_mp - 1)),
-            dma((LAYERS, n_mp - 1)),
-            dma((LAYERS, n_dp - 1)),
-            dma((LAYERS, n_dp - 1)),
+            dma((LAYERS,)),
+            dma((LAYERS,)),
+            dma((LAYERS, n_mp // 2, n_dp)),
+            dma((LAYERS, n_mp // 2, n_dp)),
             dma((LAYERS, n_mp // 2)),
             dma((LAYERS, n_mp // 2)),
             dma((LAYERS, n_mp // 2, n_mp // 2 - 1)),

time: 69.7 us -> 68.8 us (0.987)
  Pallas kernels: 67.6 us -> 66.7 us
    pallas_call x1, Pallas kernels: 67.6 us -> 66.7 us  [fused(): pl.pallas_call(functools.partial(fused_kernel, sizes), out_shape=jax.Shap...]
where the time goes in v3:
time: 68.8 us; the launch traced here: 68.4 us
  Pallas kernels  66.7 us (97%)
  local copies, waits for them, and re-layouts  1.67 us (2%)
    pallas_call x1, Pallas kernels, fused(): pl.pallas_call(functools.partial(fused_kernel, sizes), out_shape=jax.Shap...  66.7 us
    unnamed x1, local copies, waits for them, and re-layouts  1.67 us

profile of v3, /device:TPU:0, one launch (start us, length us, event | category | flops | bytes accessed | tf_op | source)
XLA Modules:
  0.0 68.4 jit_solution(14019758428423612832)
XLA Ops:
  0.0 66.7 %shard_map.100 = bf16[64,2048]{1,0:T(8,128)(2,1)} custom-call(s32[64]{0:T(128)} %slot_s.1, s32[64]{0:T(128)} %length_s.1, s32[64]{0:T(128)} %position_s.1, s32[1,64]{1,0:T(1,128)} %bitcast.3, f32[1,128]{1,0:T(1,128)} %constant.2.clone.frequency_ref, bf16[64,2048]{1,0:T(8,128)(2,1)} %hidden_ref.1, bf16[16,128]{1,0:T(8,128)(2,1)} %bitcast.2, ...), custom_call_target="tpu_custom_call" | custom-call | tf_op jit(solution)/shard_map/pallas_call | solution.py:558
  66.7 1.7 %copy.12 = bf16[64,2048]{1,0:T(8,128)(2,1)} copy(bf16[64,2048]{1,0:T(8,128)(2,1)} %shard_map.100) | data formatting | bytes 524288
